TPU v7x, 512 devices: a whole 4x8x8 slice. The times are simulated.
512 devices in a mesh: seq: 128 (over y, z, core), head: 4 (over x).
Axes of the slice: x: 4, y: 8, z: 8, core: 2. Of those that a mesh axis runs over, the one named last changes fastest.
Arguments:
- queries: bfloat16 [16384, 4096], P('seq', 'head'), may hold values from -6 to 6
- keys: bfloat16 [16384, 4096], P('seq', 'head'), may hold values from -6 to 6
- values: bfloat16 [16384, 4096], P('seq', 'head'), may hold values from -6 to 6
- hidden: bfloat16 [16384, 2048], P('seq', 'head'), may hold values from -6 to 6
- gate_weight: bfloat16 [2048, 256], P('head'), may hold values from -0.125 to 0.125
- level_slot: int32 [8], replicated, may hold values from 0 to 7, each once
- out_grad: bfloat16 [16384, 4096], P('seq', 'head'), may hold values from -6 to 6
Outputs:
- mixed: bfloat16 [16384, 4096], P('seq', 'head')
- grad_queries: bfloat16 [16384, 4096], P('seq', 'head')
- grad_keys: bfloat16 [16384, 4096], P('seq', 'head')
- grad_values: bfloat16 [16384, 4096], P('seq', 'head')
- grad_hidden: bfloat16 [16384, 2048], P('seq', 'head')
Inputs may be any that keep to these rules, and one draw needn't show every extreme that they name: `level_slot`: each column index of a head's block appears once.
All inputs are finite; a program needn't handle non-finite values.
Results may differ from a plain program's by a relative error of at most 0.01.
Values may be sent and summed in bfloat16 or wider, within the bound.
No kernel may reach another device: no remote copies, remote signals or barrier semaphores. Data moves between devices by JAX's collectives and lax.ppermute only.
A program may use at most 64 MiB of HBM per device.

v0:
```python
import jax
import jax.numpy as jnp
from jax import lax
from jax.sharding import PartitionSpec as P

DK = 128
SPAN = 128
HIGH = lax.Precision.HIGHEST


def from_partner(block, axis, stride):
    count = lax.axis_size(axis)
    route = []
    for low in range(count):
        high = low | 1 << stride
        if high != low and high < count:
            route += [(low, high), (high, low)]
    return lax.ppermute(block, axis, route)


def local(queries, keys, values, hidden, gate_weight, level_slot, out_grad):
    tok_rows = queries.shape[0]
    heads_here = queries.shape[1] // DK
    levels = level_slot.shape[0]
    rows_here = heads_here * levels
    span_count = tok_rows // SPAN
    local_bits = span_count.bit_length() - 1
    device_bits = lax.axis_size("seq").bit_length() - 1
    seq_index = lax.axis_index("seq")
    weight_cols = lax.all_to_all(gate_weight, "head", split_axis=1, concat_axis=0, tiled=True)
    logits = lax.dot_general(
        weight_cols,
        lax.all_gather(hidden, "head", axis=1, tiled=True),
        (((0,), (1,)), ((), ())),
        preferred_element_type=jnp.float32,
    )
    slot_table = (level_slot[:, None] == jnp.arange(levels, dtype=jnp.int32)[None, :]).astype(
        jnp.float32
    )
    chosen = jnp.einsum(
        "lm,hmt->hlt", slot_table, logits.reshape(heads_here, levels, tok_rows), precision=HIGH
    )
    weights = jnp.transpose(jax.nn.softplus(chosen), (2, 0, 1))
    query_heads = queries.reshape(tok_rows, heads_here, DK)
    grad_heads = out_grad.reshape(tok_rows, heads_here, DK)
    query_blocks = queries.reshape(span_count, SPAN, heads_here, DK)
    key_blocks = keys.reshape(span_count, SPAN, heads_here, DK)
    value_blocks = values.reshape(span_count, SPAN, heads_here, DK)
    position = jnp.arange(SPAN)
    causal = (position[:, None] >= position[None, :]).astype(jnp.float32)
    scores = jnp.einsum(
        "nchd,nshd->nhcs", query_blocks, key_blocks, preferred_element_type=jnp.float32
    )
    attend = (scores * causal / SPAN).astype(jnp.bfloat16)
    intra = jnp.einsum(
        "nhcs,nshe->nche", attend, value_blocks, preferred_element_type=jnp.float32
    ).reshape(tok_rows, heads_here, DK)
    weighted = (weights[..., None] * grad_heads[:, :, None, :]).astype(jnp.bfloat16)
    device_grads = jnp.einsum(
        "thd,thje->hjde",
        query_heads,
        weighted[:, :, 1 + local_bits :],
        preferred_element_type=jnp.float32,
    )
    span_states = jnp.einsum(
        "nchd,nche->nhde", key_blocks, value_blocks, preferred_element_type=jnp.float32
    )
    device_state = span_states.sum(0)
    group = device_state
    lower_states = []
    for bit_pos in range(device_bits):
        partner = from_partner(group.astype(jnp.bfloat16), "seq", bit_pos).astype(group.dtype)
        upper_half = seq_index >> bit_pos & 1
        lower_states.append(
            jnp.where(upper_half == 1, partner, 0.0) / float((1 << bit_pos) * tok_rows)
        )
        group = group + partner
    pending = device_grads
    carried = jnp.zeros_like(device_state)
    for bit_pos in range(device_bits):
        partner_pending = from_partner(pending.astype(jnp.bfloat16), "seq", bit_pos).astype(
            pending.dtype
        )
        upper_half = seq_index >> bit_pos & 1
        scale_here = float((1 << bit_pos) * tok_rows)
        carried = carried + jnp.where(upper_half == 0, partner_pending[:, 0], 0.0) / scale_here
        pending = pending[:, 1:] + partner_pending[:, 1:]
    device_level = jnp.stack(lower_states, 1).astype(jnp.bfloat16)
    device_outs = jnp.einsum(
        "thd,hjde->tjhe", query_heads, device_level, preferred_element_type=jnp.float32
    )
    mixed = weights[:, :, 0:1] * intra + jnp.einsum(
        "thj,tjhe->the", weights[:, :, 1:], device_outs, precision=HIGH
    )
    first_grad = jnp.sum(grad_heads * intra, -1)
    later_grad = jnp.einsum(
        "the,tjhe->thj", grad_heads.astype(jnp.float32), device_outs, precision=HIGH
    )
    weight_grad = jnp.concatenate([first_grad[:, :, None], later_grad], 2)
    first_blocks = weighted[:, :, 0].reshape(span_count, SPAN, heads_here, DK)
    grad_score = (
        jnp.einsum(
            "nche,nshe->nhcs", first_blocks, value_blocks, preferred_element_type=jnp.float32
        )
        * causal
        / SPAN
    ).astype(jnp.bfloat16)
    grad_query = jnp.einsum(
        "nhcs,nshd->nchd", grad_score, key_blocks, preferred_element_type=jnp.float32
    ).reshape(tok_rows, heads_here, DK)
    grad_key = jnp.einsum(
        "nhcs,nchd->nshd", grad_score, query_blocks, preferred_element_type=jnp.float32
    ).reshape(tok_rows, heads_here, DK)
    grad_value = jnp.einsum(
        "nhcs,nche->nshe", attend, first_blocks, preferred_element_type=jnp.float32
    ).reshape(tok_rows, heads_here, DK)
    device_back = jnp.einsum(
        "the,hjde->tjhd", grad_heads, device_level, preferred_element_type=jnp.float32
    )
    grad_query = grad_query + jnp.einsum(
        "thj,tjhd->thd", weights[:, :, 1 + local_bits :], device_back, precision=HIGH
    )
    state_total = carried[None].astype(jnp.bfloat16)
    grad_key = grad_key + jnp.einsum(
        "nche,nhde->nchd", value_blocks, state_total, preferred_element_type=jnp.float32
    ).reshape(tok_rows, heads_here, DK)
    grad_value = grad_value + jnp.einsum(
        "nchd,nhde->nche", key_blocks, state_total, preferred_element_type=jnp.float32
    ).reshape(tok_rows, heads_here, DK)
    chosen_grad = jnp.transpose(weight_grad, (1, 2, 0)) * jax.nn.sigmoid(chosen)
    logit_grad = (
        jnp.einsum("lm,hlt->hmt", slot_table, chosen_grad, precision=HIGH)
        .reshape(rows_here, tok_rows)
        .astype(jnp.bfloat16)
    )
    partial_grad = lax.dot_general(
        logit_grad, weight_cols, (((0,), (1,)), ((), ())), preferred_element_type=jnp.float32
    )
    grad_hidden = lax.psum_scatter(partial_grad, "head", scatter_dimension=1, tiled=True)
    width_all = heads_here * DK
    return (
        mixed.reshape(tok_rows, width_all).astype(jnp.bfloat16),
        grad_query.reshape(tok_rows, width_all).astype(jnp.bfloat16),
        grad_key.reshape(tok_rows, width_all).astype(jnp.bfloat16),
        grad_value.reshape(tok_rows, width_all).astype(jnp.bfloat16),
        grad_hidden.astype(jnp.bfloat16),
    )


def solution(mesh):
    placed = (
        P("seq", "head"),
        P("seq", "head"),
        P("seq", "head"),
        P("seq", "head"),
        P("head", None),
        P(),
        P("seq", "head"),
    )
    return jax.shard_map(
        local,
        mesh=mesh,
        in_specs=placed,
        out_specs=(
            P("seq", "head"),
            P("seq", "head"),
            P("seq", "head"),
            P("seq", "head"),
            P("seq", "head"),
        ),
        check_vma=False,
    )
```

profile of v0, /device:TPU:1, one launch (start us, length us, event | category | flops | bytes accessed | tf_op | source)
XLA Modules:
  0.0 322.8 jit_solution(2008449599605130262)
XLA Ops:
  7.2 1.9 copy.36
  9.1 4.8 %all-to-all-start = ((bf16[512,4,64]{0,2,1:T(8,128)(2,1)}), bf16[512,4,64]{0,2,1:T(8,128)(2,1)S(1)}, u32[]{:S(2)}, u32[]{:S(2)}) async-start(bf16[512,4,64]{0,2,1:T(8,128)(2,1)} %bitcast.3), calls=%async_computation | async-start | bytes 524288 | tf_op jit(solution)/shard_map/all_to_all | solution.py:30
  16.4 12.0 %all_gather.3 = bf16[128,2048]{1,0:T(8,128)(2,1)S(1)} all-gather(bf16[128,512]{1,0:T(8,128)(2,1)S(1)} %copy-done.34), channel_id=1, replica_groups=mesh['seq'=128,'head'=4] {'head'}, dimensions={1}, use_global_device_ids=true | all-gather | bytes 655360 | tf_op jit(solution)/shard_map/all_gather | solution.py:33
  30.3 3.2 fusion.114
  33.5 9.3 %collective-permute-start.7 = (bf16[8,7,128,128]{2,3,1,0:T(8,128)(2,1)}, bf16[8,7,128,128]{2,3,1,0:T(8,128)(2,1)}, u32[]{:S(2)}, u32[]{:S(2)}) collective-permute-start(bf16[8,7,128,128]{2,3,1,0:T(8,128)(2,1)} %get-tuple-element.35), channel_id=1, source_target_pairs={{0,4},{4,0},{8,12},{12,8},{16,20},{20,16},{24,28},{28,24},{32,36},... | collective-permute-start | bytes 5505032 | tf_op jit(solution)/shard_map/ppermute | solution.py:18
  43.8 1.9 collective-permute-start
  47.3 2.2 collective-permute-start.1
  49.5 1.9 convert_element_type.195
  51.5 3.3 %fusion.111 = (bf16[8,6,128,128]{2,3,1,0:T(8,128)(2,1)}, f32[8,6,128,128]{2,3,1,0:T(8,128)}) fusion(f32[8,7,128,128]{2,3,1,0:T(8,128)S(1)} %convert_element_type.195, f32[8,7,128,128]{2,3,1,0:T(8,128)S(1)} %copy-done.2), kind=kLoop, calls=%fused_computation.155 | loop fusion | flops 1572864 | bytes 11010048 | tf_op jit(solution)/shard_map/convert_element_type | solution.py:81
  54.7 3.4 %collective-permute-start.8 = (bf16[8,6,128,128]{2,3,1,0:T(8,128)(2,1)}, bf16[8,6,128,128]{2,3,1,0:T(8,128)(2,1)}, u32[]{:S(2)}, u32[]{:S(2)}) collective-permute-start(bf16[8,6,128,128]{2,3,1,0:T(8,128)(2,1)} %get-tuple-element.23), channel_id=1, source_target_pairs={{0,8},{8,0},{4,12},{12,4},{16,24},{24,16},{20,28},{28,20},{32,40},... | collective-permute-start | bytes 4718600 | tf_op jit(solution)/shard_map/ppermute | solution.py:18
  58.2 1.9 collective-permute-start.2
  60.8 36.5 %collective-permute-done.2 = bf16[8,128,128]{2,1,0:T(8,128)(2,1)S(1)} collective-permute-done((bf16[8,128,128]{2,1,0:T(8,128)(2,1)S(1)}, bf16[8,128,128]{2,1,0:T(8,128)(2,1)S(1)}, u32[]{:S(2)}, u32[]{:S(2)}) %collective-permute-start.2) | collective-permute-done | bytes 262176 | tf_op jit(solution)/shard_map/ppermute | solution.py:18
  97.4 5.9 %collective-permute-start.3 = (bf16[8,128,128]{2,1,0:T(8,128)(2,1)S(1)}, bf16[8,128,128]{2,1,0:T(8,128)(2,1)S(1)}, u32[]{:S(2)}, u32[]{:S(2)}) collective-permute-start(bf16[8,128,128]{2,1,0:T(8,128)(2,1)S(1)} %fusion.47), channel_id=1, source_target_pairs={{0,32},{32,0},{4,36},{36,4},{8,40},{40,8},{12,44},{44,12},{16,48},... | collective-permute-start | bytes 786440 | tf_op jit(solution)/shard_map/ppermute | solution.py:18
  103.5 6.3 %collective-permute-done.3 = bf16[8,128,128]{2,1,0:T(8,128)(2,1)S(1)} collective-permute-done((bf16[8,128,128]{2,1,0:T(8,128)(2,1)S(1)}, bf16[8,128,128]{2,1,0:T(8,128)(2,1)S(1)}, u32[]{:S(2)}, u32[]{:S(2)}) %collective-permute-start.3) | collective-permute-done | bytes 262176 | tf_op jit(solution)/shard_map/ppermute | solution.py:18
  110.0 2.4 collective-permute-start.4
  114.7 11.1 %collective-permute-start.9 = (bf16[8,5,128,128]{2,3,1,0:T(8,128)(2,1)S(1)}, bf16[8,5,128,128]{2,3,1,0:T(8,128)(2,1)S(1)}, u32[]{:S(2)}, u32[]{:S(2)}) collective-permute-start(bf16[8,5,128,128]{2,3,1,0:T(8,128)(2,1)S(1)} %get-tuple-element.21), channel_id=1, source_target_pairs={{0,16},{16,0},{4,20},{20,4},{8,24},{24,8},{12,28},{28,12},{32,48},... | collective-permute-start | bytes 3932168 | tf_op jit(solution)/shard_map/ppermute | solution.py:18
  125.9 4.1 %collective-permute-start.5 = (bf16[8,128,128]{2,1,0:T(8,128)(2,1)S(1)}, bf16[8,128,128]{2,1,0:T(8,128)(2,1)S(1)}, u32[]{:S(2)}, u32[]{:S(2)}) collective-permute-start(bf16[8,128,128]{2,1,0:T(8,128)(2,1)S(1)} %fusion.48), channel_id=1, source_target_pairs={{0,128},{128,0},{4,132},{132,4},{8,136},{136,8},{12,140},{140,12},... | collective-permute-start | bytes 786440 | tf_op jit(solution)/shard_map/ppermute | solution.py:18
  130.3 11.1 %collective-permute-done.5 = bf16[8,128,128]{2,1,0:T(8,128)(2,1)S(1)} collective-permute-done((bf16[8,128,128]{2,1,0:T(8,128)(2,1)S(1)}, bf16[8,128,128]{2,1,0:T(8,128)(2,1)S(1)}, u32[]{:S(2)}, u32[]{:S(2)}) %collective-permute-start.5) | collective-permute-done | bytes 262176 | tf_op jit(solution)/shard_map/ppermute | solution.py:18
  141.5 6.8 %collective-permute-start.6 = (bf16[8,128,128]{2,1,0:T(8,128)(2,1)S(1)}, bf16[8,128,128]{2,1,0:T(8,128)(2,1)S(1)}, u32[]{:S(2)}, u32[]{:S(2)}) collective-permute-start(bf16[8,128,128]{2,1,0:T(8,128)(2,1)S(1)} %fusion.29), channel_id=1, source_target_pairs={{0,256},{256,0},{4,260},{260,4},{8,264},{264,8},{12,268},{268,12},... | collective-permute-start | bytes 786440 | tf_op jit(solution)/shard_map/ppermute | solution.py:18
  148.5 33.7 %collective-permute-done.9 = bf16[8,5,128,128]{2,3,1,0:T(8,128)(2,1)S(1)} collective-permute-done((bf16[8,5,128,128]{2,3,1,0:T(8,128)(2,1)S(1)}, bf16[8,5,128,128]{2,3,1,0:T(8,128)(2,1)S(1)}, u32[]{:S(2)}, u32[]{:S(2)}) %collective-permute-start.9) | collective-permute-done | bytes 1310752 | tf_op jit(solution)/shard_map/ppermute | solution.py:18
  184.0 6.3 %collective-permute-start.10 = (bf16[8,4,128,128]{2,3,1,0:T(8,128)(2,1)S(1)}, bf16[8,4,128,128]{2,3,1,0:T(8,128)(2,1)S(1)}, u32[]{:S(2)}, u32[]{:S(2)}) collective-permute-start(bf16[8,4,128,128]{2,3,1,0:T(8,128)(2,1)S(1)} %get-tuple-element.19), channel_id=1, source_target_pairs={{0,32},{32,0},{4,36},{36,4},{8,40},{40,8},{12,44},{44,12},{16,48},... | collective-permute-start | bytes 3145736 | tf_op jit(solution)/shard_map/ppermute | solution.py:18
  193.4 42.9 %collective-permute-done.10 = bf16[8,4,128,128]{2,3,1,0:T(8,128)(2,1)S(1)} collective-permute-done((bf16[8,4,128,128]{2,3,1,0:T(8,128)(2,1)S(1)}, bf16[8,4,128,128]{2,3,1,0:T(8,128)(2,1)S(1)}, u32[]{:S(2)}, u32[]{:S(2)}) %collective-permute-start.10) | collective-permute-done | bytes 1048608 | tf_op jit(solution)/shard_map/ppermute | solution.py:18
  236.5 1.8 fusion.108
  238.6 3.7 %collective-permute-start.11 = (bf16[8,3,128,128]{2,3,1,0:T(8,128)(2,1)}, bf16[8,3,128,128]{2,3,1,0:T(8,128)(2,1)}, u32[]{:S(2)}, u32[]{:S(2)}) collective-permute-start(bf16[8,3,128,128]{2,3,1,0:T(8,128)(2,1)} %get-tuple-element.17), channel_id=1, source_target_pairs={{0,64},{64,0},{4,68},{68,4},{8,72},{72,8},{12,76},{76,12},{16,80},... | collective-permute-start | bytes 2359304 | tf_op jit(solution)/shard_map/ppermute | solution.py:18
  243.8 14.9 %collective-permute-done.11 = bf16[8,3,128,128]{2,3,1,0:T(8,128)(2,1)} collective-permute-done((bf16[8,3,128,128]{2,3,1,0:T(8,128)(2,1)}, bf16[8,3,128,128]{2,3,1,0:T(8,128)(2,1)}, u32[]{:S(2)}, u32[]{:S(2)}) %collective-permute-start.11) | collective-permute-done | bytes 786464 | tf_op jit(solution)/shard_map/ppermute | solution.py:18
  262.5 3.0 collective-permute-start.12
  267.0 2.3 fusion.74
  269.2 20.1 %collective-permute-done.12 = bf16[8,2,128,128]{2,3,1,0:T(8,128)(2,1)} collective-permute-done((bf16[8,2,128,128]{2,3,1,0:T(8,128)(2,1)}, bf16[8,2,128,128]{2,3,1,0:T(8,128)(2,1)}, u32[]{:S(2)}, u32[]{:S(2)}) %collective-permute-start.12) | collective-permute-done | bytes 524320 | tf_op jit(solution)/shard_map/ppermute | solution.py:18
  292.3 6.1 %collective-permute-start.13 = (bf16[8,1,128,128]{2,3,1,0:T(8,128)(2,1)}, bf16[8,1,128,128]{2,3,1,0:T(8,128)(2,1)}, u32[]{:S(2)}, u32[]{:S(2)}) collective-permute-start(bf16[8,1,128,128]{2,3,1,0:T(8,128)(2,1)} %fusion.30), channel_id=1, source_target_pairs={{0,256},{256,0},{4,260},{260,4},{8,264},{264,8},{12,268},{268,12},... | collective-permute-start | bytes 786440 | tf_op jit(solution)/shard_map/ppermute | solution.py:18
  302.2 1.8 copy.58
  305.6 5.6 %collective-permute-done.13 = bf16[8,1,128,128]{2,3,1,0:T(8,128)(2,1)} collective-permute-done((bf16[8,1,128,128]{2,3,1,0:T(8,128)(2,1)}, bf16[8,1,128,128]{2,3,1,0:T(8,128)(2,1)}, u32[]{:S(2)}, u32[]{:S(2)}) %collective-permute-start.13) | collective-permute-done | bytes 262176 | tf_op jit(solution)/shard_map/ppermute | solution.py:18
  311.2 2.1 fusion.34
  (136 shorter events, 33.6 us)
Async XLA Ops:
  7.2 35.9 %copy-start = (bf16[128,1024]{1,0:T(8,128)(2,1)S(1)}, bf16[128,1024]{1,0:T(8,128)(2,1)}, u32[]{:S(2)}) copy-start(bf16[128,1024]{1,0:T(8,128)(2,1)} %param.9) | copy-start | bytes 786436
  7.2 9.2 %copy-start.34 = (bf16[128,512]{1,0:T(8,128)(2,1)S(1)}, bf16[128,512]{1,0:T(8,128)(2,1)}, u32[]{:S(2)}) copy-start(bf16[128,512]{1,0:T(8,128)(2,1)} %param.10) | copy-start | bytes 393220
  9.1 19.4 %all-to-all-start = ((bf16[512,4,64]{0,2,1:T(8,128)(2,1)}), bf16[512,4,64]{0,2,1:T(8,128)(2,1)S(1)}, u32[]{:S(2)}, u32[]{:S(2)}) async-start(bf16[512,4,64]{0,2,1:T(8,128)(2,1)} %bitcast.3), calls=%async_computation | async-start | bytes 524288 | tf_op jit(solution)/shard_map/all_to_all | solution.py:30
  13.9 290.1 %reduce-scatter.2.cloned.1.call-start = ((), (), s32[]{:S(2)}) async-start(), calls=%async_computation.2 | async-start | bytes 1310720 | tf_op jit(solution)/shard_map/reduce_scatter | solution.py:139
  15.0 13.7 %copy-start.25 = (bf16[128,1024]{0,1:T(8,128)(2,1)}, bf16[128,1024]{0,1:T(8,128)(2,1)S(1)}, u32[]{:S(2)}) copy-start(bf16[128,1024]{0,1:T(8,128)(2,1)S(1)} %copy.47) | copy-start | bytes 786436
  15.0 13.7 %copy-start.35 = (s32[8]{0:T(128)S(1)}, s32[8]{0:T(128)}, u32[]{:S(2)}) copy-start(s32[8]{0:T(128)} %param.12) | copy-start | bytes 100
  16.1 44.0 %copy-start.12 = (bf16[16,8,8,128]{3,2,1,0:T(8,128)(2,1)}, bf16[16,8,8,128]{3,2,1,0:T(8,128)(2,1)S(1)}, u32[]{:S(2)}) copy-start(bf16[16,8,8,128]{3,2,1,0:T(8,128)(2,1)S(1)} %copy.101) | copy-start | bytes 786436
  16.2 14.1 %copy-start.8 = (f32[128,8,128]{0,2,1:T(8,128)}, f32[128,8,128]{0,2,1:T(8,128)S(1)}, u32[]{:S(2)}) copy-start(f32[128,8,128]{0,2,1:T(8,128)S(1)} %bitcast_convert_fusion) | copy-start | bytes 1572868
  30.3 12.5 %copy-start.19 = (bf16[128,1024]{1,0:T(8,128)(2,1)S(1)}, bf16[128,1024]{1,0:T(8,128)(2,1)}, u32[]{:S(2)}) copy-start(bf16[128,1024]{1,0:T(8,128)(2,1)} %param.8) | copy-start | bytes 786436
  33.5 16.0 %collective-permute-start.7 = (bf16[8,7,128,128]{2,3,1,0:T(8,128)(2,1)}, bf16[8,7,128,128]{2,3,1,0:T(8,128)(2,1)}, u32[]{:S(2)}, u32[]{:S(2)}) collective-permute-start(bf16[8,7,128,128]{2,3,1,0:T(8,128)(2,1)} %get-tuple-element.35), channel_id=1, source_target_pairs={{0,4},{4,0},{8,12},{12,8},{16,20},{20,16},{24,28},{28,24},{32,36},... | collective-permute-start | bytes 5505032 | tf_op jit(solution)/shard_map/ppermute | solution.py:18
  43.8 3.4 %collective-permute-start = (bf16[8,128,128]{2,1,0:T(8,128)(2,1)S(1)}, bf16[8,128,128]{2,1,0:T(8,128)(2,1)S(1)}, u32[]{:S(2)}, u32[]{:S(2)}) collective-permute-start(bf16[8,128,128]{2,1,0:T(8,128)(2,1)S(1)} %get-tuple-element.29), channel_id=1, source_target_pairs={{0,4},{4,0},{8,12},{12,8},{16,20},{20,16},{24,28},{28,24},{32,36},... | collective-permute-start | bytes 786440 | tf_op jit(solution)/shard_map/ppermute | solution.py:18
  47.3 10.8 %collective-permute-start.1 = (bf16[8,128,128]{2,1,0:T(8,128)(2,1)S(1)}, bf16[8,128,128]{2,1,0:T(8,128)(2,1)S(1)}, u32[]{:S(2)}, u32[]{:S(2)}) collective-permute-start(bf16[8,128,128]{2,1,0:T(8,128)(2,1)S(1)} %fusion.46), channel_id=1, source_target_pairs={{0,8},{8,0},{4,12},{12,4},{16,24},{24,16},{20,28},{28,20},{32,40},... | collective-permute-start | bytes 786440 | tf_op jit(solution)/shard_map/ppermute | solution.py:18
  54.7 57.6 %collective-permute-start.8 = (bf16[8,6,128,128]{2,3,1,0:T(8,128)(2,1)}, bf16[8,6,128,128]{2,3,1,0:T(8,128)(2,1)}, u32[]{:S(2)}, u32[]{:S(2)}) collective-permute-start(bf16[8,6,128,128]{2,3,1,0:T(8,128)(2,1)} %get-tuple-element.23), channel_id=1, source_target_pairs={{0,8},{8,0},{4,12},{12,4},{16,24},{24,16},{20,28},{28,20},{32,40},... | collective-permute-start | bytes 4718600 | tf_op jit(solution)/shard_map/ppermute | solution.py:18
  58.2 39.0 %collective-permute-start.2 = (bf16[8,128,128]{2,1,0:T(8,128)(2,1)S(1)}, bf16[8,128,128]{2,1,0:T(8,128)(2,1)S(1)}, u32[]{:S(2)}, u32[]{:S(2)}) collective-permute-start(bf16[8,128,128]{2,1,0:T(8,128)(2,1)S(1)} %fusion.106), channel_id=1, source_target_pairs={{0,16},{16,0},{4,20},{20,4},{8,24},{24,8},{12,28},{28,12},{32,48},... | collective-permute-start | bytes 786440 | tf_op jit(solution)/shard_map/ppermute | solution.py:18
  60.4 49.5 %copy-start.21 = (bf16[128,8,128]{0,2,1:T(8,128)(2,1)}, bf16[128,8,128]{0,2,1:T(8,128)(2,1)S(1)}, u32[]{:S(2)}) copy-start(bf16[128,8,128]{0,2,1:T(8,128)(2,1)S(1)} %copy.51) | copy-start | bytes 786436
  60.8 131.0 %copy-start.30 = (bf16[8,128,128]{2,1,0:T(8,128)(2,1)}, bf16[8,128,128]{2,1,0:T(8,128)(2,1)S(1)}, u32[]{:S(2)}) copy-start(bf16[8,128,128]{2,1,0:T(8,128)(2,1)S(1)} %fusion.11) | copy-start | bytes 786436
  97.2 12.7 %copy-start.23 = (bf16[8,128,128]{2,1,0:T(8,128)(2,1)}, bf16[8,128,128]{2,1,0:T(8,128)(2,1)S(1)}, u32[]{:S(2)}) copy-start(bf16[8,128,128]{2,1,0:T(8,128)(2,1)S(1)} %collective-permute-done.2) | copy-start | bytes 786436
  97.4 12.4 %collective-permute-start.3 = (bf16[8,128,128]{2,1,0:T(8,128)(2,1)S(1)}, bf16[8,128,128]{2,1,0:T(8,128)(2,1)S(1)}, u32[]{:S(2)}, u32[]{:S(2)}) collective-permute-start(bf16[8,128,128]{2,1,0:T(8,128)(2,1)S(1)} %fusion.47), channel_id=1, source_target_pairs={{0,32},{32,0},{4,36},{36,4},{8,40},{40,8},{12,44},{44,12},{16,48},... | collective-permute-start | bytes 786440 | tf_op jit(solution)/shard_map/ppermute | solution.py:18
  110.0 15.9 %collective-permute-start.4 = (bf16[8,128,128]{2,1,0:T(8,128)(2,1)S(1)}, bf16[8,128,128]{2,1,0:T(8,128)(2,1)S(1)}, u32[]{:S(2)}, u32[]{:S(2)}) collective-permute-start(bf16[8,128,128]{2,1,0:T(8,128)(2,1)S(1)} %get-tuple-element.25), channel_id=1, source_target_pairs={{0,64},{64,0},{4,68},{68,4},{8,72},{72,8},{12,76},{76,12},{16,80},... | collective-permute-start | bytes 786440 | tf_op jit(solution)/shard_map/ppermute | solution.py:18
  114.1 11.6 %copy-start.24 = (bf16[8,128,128]{2,1,0:T(8,128)(2,1)S(1)}, bf16[8,128,128]{2,1,0:T(8,128)(2,1)}, u32[]{:S(2)}) copy-start(bf16[8,128,128]{2,1,0:T(8,128)(2,1)} %copy-done.23) | copy-start | bytes 786436
  114.7 67.5 %collective-permute-start.9 = (bf16[8,5,128,128]{2,3,1,0:T(8,128)(2,1)S(1)}, bf16[8,5,128,128]{2,3,1,0:T(8,128)(2,1)S(1)}, u32[]{:S(2)}, u32[]{:S(2)}) collective-permute-start(bf16[8,5,128,128]{2,3,1,0:T(8,128)(2,1)S(1)} %get-tuple-element.21), channel_id=1, source_target_pairs={{0,16},{16,0},{4,20},{20,4},{8,24},{24,8},{12,28},{28,12},{32,48},... | collective-permute-start | bytes 3932168 | tf_op jit(solution)/shard_map/ppermute | solution.py:18
  125.9 15.5 %collective-permute-start.5 = (bf16[8,128,128]{2,1,0:T(8,128)(2,1)S(1)}, bf16[8,128,128]{2,1,0:T(8,128)(2,1)S(1)}, u32[]{:S(2)}, u32[]{:S(2)}) collective-permute-start(bf16[8,128,128]{2,1,0:T(8,128)(2,1)S(1)} %fusion.48), channel_id=1, source_target_pairs={{0,128},{128,0},{4,132},{132,4},{8,136},{136,8},{12,140},{140,12},... | collective-permute-start | bytes 786440 | tf_op jit(solution)/shard_map/ppermute | solution.py:18
  141.5 48.8 %collective-permute-start.6 = (bf16[8,128,128]{2,1,0:T(8,128)(2,1)S(1)}, bf16[8,128,128]{2,1,0:T(8,128)(2,1)S(1)}, u32[]{:S(2)}, u32[]{:S(2)}) collective-permute-start(bf16[8,128,128]{2,1,0:T(8,128)(2,1)S(1)} %fusion.29), channel_id=1, source_target_pairs={{0,256},{256,0},{4,260},{260,4},{8,264},{264,8},{12,268},{268,12},... | collective-permute-start | bytes 786440 | tf_op jit(solution)/shard_map/ppermute | solution.py:18
  184.0 52.3 %collective-permute-start.10 = (bf16[8,4,128,128]{2,3,1,0:T(8,128)(2,1)S(1)}, bf16[8,4,128,128]{2,3,1,0:T(8,128)(2,1)S(1)}, u32[]{:S(2)}, u32[]{:S(2)}) collective-permute-start(bf16[8,4,128,128]{2,3,1,0:T(8,128)(2,1)S(1)} %get-tuple-element.19), channel_id=1, source_target_pairs={{0,32},{32,0},{4,36},{36,4},{8,40},{40,8},{12,44},{44,12},{16,48},... | collective-permute-start | bytes 3145736 | tf_op jit(solution)/shard_map/ppermute | solution.py:18
  238.6 20.1 %collective-permute-start.11 = (bf16[8,3,128,128]{2,3,1,0:T(8,128)(2,1)}, bf16[8,3,128,128]{2,3,1,0:T(8,128)(2,1)}, u32[]{:S(2)}, u32[]{:S(2)}) collective-permute-start(bf16[8,3,128,128]{2,3,1,0:T(8,128)(2,1)} %get-tuple-element.17), channel_id=1, source_target_pairs={{0,64},{64,0},{4,68},{68,4},{8,72},{72,8},{12,76},{76,12},{16,80},... | collective-permute-start | bytes 2359304 | tf_op jit(solution)/shard_map/ppermute | solution.py:18
  243.8 17.4 %copy-start.10 = (f32[8,3,128,128]{2,3,1,0:T(8,128)S(1)}, f32[8,3,128,128]{2,3,1,0:T(8,128)}, u32[]{:S(2)}) copy-start(f32[8,3,128,128]{2,3,1,0:T(8,128)} %get-tuple-element.18) | copy-start | bytes 4718596
  262.5 26.8 %collective-permute-start.12 = (bf16[8,2,128,128]{2,3,1,0:T(8,128)(2,1)}, bf16[8,2,128,128]{2,3,1,0:T(8,128)(2,1)}, u32[]{:S(2)}, u32[]{:S(2)}) collective-permute-start(bf16[8,2,128,128]{2,3,1,0:T(8,128)(2,1)} %get-tuple-element.15), channel_id=1, source_target_pairs={{0,128},{128,0},{4,132},{132,4},{8,136},{136,8},{12,140},{140,12},... | collective-permute-start | bytes 1572872 | tf_op jit(solution)/shard_map/ppermute | solution.py:18
  265.6 25.9 %copy-start.16 = (f32[8,2,128,128]{2,3,1,0:T(8,128)S(1)}, f32[8,2,128,128]{2,3,1,0:T(8,128)}, u32[]{:S(2)}) copy-start(f32[8,2,128,128]{2,3,1,0:T(8,128)} %get-tuple-element.16) | copy-start | bytes 3145732
  266.9 32.1 %copy-start.32 = (bf16[8,128,128]{2,1,0:T(8,128)(2,1)}, bf16[8,128,128]{2,1,0:T(8,128)(2,1)S(1)}, u32[]{:S(2)}) copy-start(bf16[8,128,128]{2,1,0:T(8,128)(2,1)S(1)} %fusion.12) | copy-start | bytes 786436
  266.9 31.5 %copy-start.15 = (bf16[8,7,128,128]{3,2,0,1:T(8,128)(2,1)S(1)}, bf16[8,7,128,128]{3,2,0,1:T(8,128)(2,1)}, u32[]{:S(2)}) copy-start(bf16[8,7,128,128]{3,2,0,1:T(8,128)(2,1)} %copy-done.14) | copy-start | bytes 5505028
  266.9 31.5 %copy-start.27 = (bf16[128,1024]{0,1:T(8,128)(2,1)S(1)}, bf16[128,1024]{0,1:T(8,128)(2,1)}, u32[]{:S(2)}) copy-start(bf16[128,1024]{0,1:T(8,128)(2,1)} %copy-done.25) | copy-start | bytes 786436
  292.3 18.9 %collective-permute-start.13 = (bf16[8,1,128,128]{2,3,1,0:T(8,128)(2,1)}, bf16[8,1,128,128]{2,3,1,0:T(8,128)(2,1)}, u32[]{:S(2)}, u32[]{:S(2)}) collective-permute-start(bf16[8,1,128,128]{2,3,1,0:T(8,128)(2,1)} %fusion.30), channel_id=1, source_target_pairs={{0,256},{256,0},{4,260},{260,4},{8,264},{264,8},{12,268},{268,12},... | collective-permute-start | bytes 786440 | tf_op jit(solution)/shard_map/ppermute | solution.py:18
  (20 other events, 65.4 us)
Sparse Core Ops, SparseCore 0:
  243.9 26.9 reduce-scatter.1
where the time goes:
time: 324 us; the launch traced here: 323 us
  waiting for transfers between devices  173 us (53%)
  starting transfers between devices  72.8 us (22%)
  other arithmetic  21.7 us (7%)
  between operations  15 us (5%)
  local copies, waits for them, and re-layouts  14.9 us (5%)
  matrix products  13.7 us (4%)
  blocking collectives  12 us (4%)
    ppermute x14, waiting for transfers between devices, from_partner(): return lax.ppermute(block, axis, route)  173 us
    ppermute x14, starting transfers between devices, from_partner(): return lax.ppermute(block, axis, route)  68 us
    unnamed x80, local copies, waits for them, and re-layouts  14.2 us
    all_gather x1, blocking collectives, local(): lax.all_gather(hidden, 'head', axis=1, tiled=True)  12 us
    convert_element_type x6, other arithmetic, local(): pending.astype(jnp.bfloat16)  8.11 us
    convert_element_type x6, other arithmetic, local(): from_partner(pending.astype(jnp.bfloat16), 'seq', bit_pos)  6.68 us
  transfers between devices with their start and end apart: 16, of which 9 were waited for; matrix products, arithmetic and copies ran while one was open for 10% of the time, Pallas kernels for 0%

commit v1 on v0

--- a/solution.py
+++ b/solution.py
@@ -28,9 +28,15 @@
     device_bits = lax.axis_size("seq").bit_length() - 1
     seq_index = lax.axis_index("seq")
     weight_cols = lax.all_to_all(gate_weight, "head", split_axis=1, concat_axis=0, tiled=True)
+    expand_the_cubes = lambda vector: jnp.concatenate(
+        jax.lax.all_to_all(
+            jnp.stack([vector for _ in range(jax.lax.axis_size("head"))], axis=0), "head", 0, 0
+        ),
+        axis=1,
+    )
     logits = lax.dot_general(
         weight_cols,
-        lax.all_gather(hidden, "head", axis=1, tiled=True),
+        expand_the_cubes(hidden),
         (((0,), (1,)), ((), ())),
         preferred_element_type=jnp.float32,
     )

time: 324 us -> 326 us (level)
  blocking collectives: 12 us -> 0 us
  starting transfers between devices: 72.8 us -> 79.3 us
  waiting for transfers between devices: 173 us -> 177 us
    all_gather x1 -> x0, blocking collectives: 12 us -> none  [local(): lax.all_gather(hidden, 'head', axis=1, tiled=True)]
    all_to_all x0 -> x1, waiting for transfers between devices: none -> 6.27 us  [local(): jax.lax.all_to_all(jnp.stack([vector for _ in range(jax.lax.axis_size('he...]
    ppermute x14, waiting for transfers between devices: 173 us -> 166 us  [from_partner(): return lax.ppermute(block, axis, route)]
    all_to_all x1, waiting for transfers between devices: 0.01 us -> 4.5 us  [local(): lax.all_to_all(gate_weight, 'head', split_axis=1, concat_axis=0, tiled=True)]
    all_to_all x0 -> x1, starting transfers between devices: none -> 3.47 us  [local(): jax.lax.all_to_all(jnp.stack([vector for _ in range(jax.lax.axis_size('he...]
    unnamed x80 -> x83, local copies, waits for them, and re-layouts: 14.2 us -> 13.3 us
  transfers between devices with their start and end apart: 16 -> 17, of which waited for: 9 -> 11; matrix products, arithmetic and copies ran while one was open for 10% -> 10% of each run, Pallas kernels for 0% -> 0%
where the time goes in v1:
time: 326 us; the launch traced here: 322 us
  waiting for transfers between devices  177 us (54%)
  starting transfers between devices  79.3 us (24%)
  other arithmetic  21.7 us (7%)
  between operations  15 us (5%)
  local copies, waits for them, and re-layouts  14.8 us (5%)
  matrix products  13.6 us (4%)
    ppermute x14, waiting for transfers between devices, from_partner(): return lax.ppermute(block, axis, route)  166 us
    ppermute x14, starting transfers between devices, from_partner(): return lax.ppermute(block, axis, route)  71 us
    unnamed x83, local copies, waits for them, and re-layouts  13.3 us
    convert_element_type x6, other arithmetic, local(): pending.astype(jnp.bfloat16)  8.1 us
    convert_element_type x6, other arithmetic, local(): from_partner(pending.astype(jnp.bfloat16), 'seq', bit_pos)  6.68 us
  transfers between devices with their start and end apart: 17, of which 11 were waited for; matrix products, arithmetic and copies ran while one was open for 10% of the time, Pallas kernels for 0%

profile of v1, /device:TPU:1, one launch (start us, length us, event | category | flops | bytes accessed | tf_op | source)
XLA Modules:
  0.0 321.7 jit_solution(4163312606137616097)
XLA Ops:
  7.2 1.9 copy.36
  9.1 4.8 %all-to-all-start = ((bf16[512,4,64]{0,2,1:T(8,128)(2,1)}), bf16[512,4,64]{0,2,1:T(8,128)(2,1)S(1)}, u32[]{:S(2)}, u32[]{:S(2)}) async-start(bf16[512,4,64]{0,2,1:T(8,128)(2,1)} %bitcast.3), calls=%async_computation | async-start | bytes 524288 | tf_op jit(solution)/shard_map/all_to_all | solution.py:30
  14.9 4.5 %all-to-all-done = bf16[512,4,64]{0,2,1:T(8,128)(2,1)S(1)} async-done(((bf16[512,4,64]{0,2,1:T(8,128)(2,1)}), bf16[512,4,64]{0,2,1:T(8,128)(2,1)S(1)}, u32[]{:S(2)}, u32[]{:S(2)}) %all-to-all-start) | async-done | bytes 262176 | tf_op jit(solution)/shard_map/all_to_all | solution.py:30
  20.3 3.5 %all-to-all-start.1 = ((bf16[4,128,512]{1,2,0:T(8,128)(2,1)}), bf16[4,128,512]{1,2,0:T(8,128)(2,1)S(1)}, u32[]{:S(2)}, u32[]{:S(2)}) async-start(bf16[4,128,512]{1,2,0:T(8,128)(2,1)} %stack.39), calls=%async_computation.1 | async-start | bytes 1048576 | tf_op jit(solution)/shard_map/all_to_all | solution.py:32
  24.4 6.3 %all-to-all-done.1 = bf16[4,128,512]{1,2,0:T(8,128)(2,1)S(1)} async-done(((bf16[4,128,512]{1,2,0:T(8,128)(2,1)}), bf16[4,128,512]{1,2,0:T(8,128)(2,1)S(1)}, u32[]{:S(2)}, u32[]{:S(2)}) %all-to-all-start.1) | async-done | bytes 524320 | tf_op jit(solution)/shard_map/all_to_all | solution.py:32
  32.5 3.2 %fusion.113 = (bf16[8,7,128,128]{2,3,1,0:T(8,128)(2,1)}, f32[8,7,128,128]{2,3,1,0:T(8,128)}) fusion(bf16[128,8,128,1]{2,1,0,3:T(8,128)(2,1)S(1)} %bitcast.212, bf16[128,8,8,128]{3,0,1,2:T(8,128)(2,1)S(1)} %multiply_convert_fusion), kind=kOutput, calls=%fused_computation.157 | convolution fusion | flops 235798528 | bytes 7602176 | tf_op jit(solution)/shard_map/thd,thje->hjde/dot_general | solution.py:65
  35.7 9.6 %collective-permute-start.7 = (bf16[8,7,128,128]{2,3,1,0:T(8,128)(2,1)}, bf16[8,7,128,128]{2,3,1,0:T(8,128)(2,1)}, u32[]{:S(2)}, u32[]{:S(2)}) collective-permute-start(bf16[8,7,128,128]{2,3,1,0:T(8,128)(2,1)} %get-tuple-element.35), channel_id=1, source_target_pairs={{0,4},{4,0},{8,12},{12,8},{16,20},{20,16},{24,28},{28,24},{32,36},... | collective-permute-start | bytes 5505032 | tf_op jit(solution)/shard_map/ppermute | solution.py:18
  46.3 1.9 collective-permute-start
  49.8 2.2 collective-permute-start.1
  52.0 1.9 convert_element_type.195
  53.9 3.3 %fusion.110 = (bf16[8,6,128,128]{2,3,1,0:T(8,128)(2,1)}, f32[8,6,128,128]{2,3,1,0:T(8,128)}) fusion(f32[8,7,128,128]{2,3,1,0:T(8,128)S(1)} %convert_element_type.195, f32[8,7,128,128]{2,3,1,0:T(8,128)S(1)} %copy-done.2), kind=kLoop, calls=%fused_computation.154 | loop fusion | flops 1572864 | bytes 11010048 | tf_op jit(solution)/shard_map/convert_element_type | solution.py:87
  57.2 3.4 %collective-permute-start.8 = (bf16[8,6,128,128]{2,3,1,0:T(8,128)(2,1)}, bf16[8,6,128,128]{2,3,1,0:T(8,128)(2,1)}, u32[]{:S(2)}, u32[]{:S(2)}) collective-permute-start(bf16[8,6,128,128]{2,3,1,0:T(8,128)(2,1)} %get-tuple-element.23), channel_id=1, source_target_pairs={{0,8},{8,0},{4,12},{12,4},{16,24},{24,16},{20,28},{28,20},{32,40},... | collective-permute-start | bytes 4718600 | tf_op jit(solution)/shard_map/ppermute | solution.py:18
  60.7 2.3 collective-permute-start.2
  63.6 36.1 %collective-permute-done.2 = bf16[8,128,128]{2,1,0:T(8,128)(2,1)S(1)} collective-permute-done((bf16[8,128,128]{2,1,0:T(8,128)(2,1)S(1)}, bf16[8,128,128]{2,1,0:T(8,128)(2,1)S(1)}, u32[]{:S(2)}, u32[]{:S(2)}) %collective-permute-start.2) | collective-permute-done | bytes 262176 | tf_op jit(solution)/shard_map/ppermute | solution.py:18
  99.9 6.5 %collective-permute-start.3 = (bf16[8,128,128]{2,1,0:T(8,128)(2,1)S(1)}, bf16[8,128,128]{2,1,0:T(8,128)(2,1)S(1)}, u32[]{:S(2)}, u32[]{:S(2)}) collective-permute-start(bf16[8,128,128]{2,1,0:T(8,128)(2,1)S(1)} %fusion.45), channel_id=1, source_target_pairs={{0,32},{32,0},{4,36},{36,4},{8,40},{40,8},{12,44},{44,12},{16,48},... | collective-permute-start | bytes 786440 | tf_op jit(solution)/shard_map/ppermute | solution.py:18
  106.6 5.7 %collective-permute-done.3 = bf16[8,128,128]{2,1,0:T(8,128)(2,1)S(1)} collective-permute-done((bf16[8,128,128]{2,1,0:T(8,128)(2,1)S(1)}, bf16[8,128,128]{2,1,0:T(8,128)(2,1)S(1)}, u32[]{:S(2)}, u32[]{:S(2)}) %collective-permute-start.3) | collective-permute-done | bytes 262176 | tf_op jit(solution)/shard_map/ppermute | solution.py:18
  112.4 3.0 collective-permute-start.4
  117.7 11.0 %collective-permute-start.9 = (bf16[8,5,128,128]{2,3,1,0:T(8,128)(2,1)S(1)}, bf16[8,5,128,128]{2,3,1,0:T(8,128)(2,1)S(1)}, u32[]{:S(2)}, u32[]{:S(2)}) collective-permute-start(bf16[8,5,128,128]{2,3,1,0:T(8,128)(2,1)S(1)} %get-tuple-element.21), channel_id=1, source_target_pairs={{0,16},{16,0},{4,20},{20,4},{8,24},{24,8},{12,28},{28,12},{32,48},... | collective-permute-start | bytes 3932168 | tf_op jit(solution)/shard_map/ppermute | solution.py:18
  128.9 4.2 %collective-permute-start.5 = (bf16[8,128,128]{2,1,0:T(8,128)(2,1)S(1)}, bf16[8,128,128]{2,1,0:T(8,128)(2,1)S(1)}, u32[]{:S(2)}, u32[]{:S(2)}) collective-permute-start(bf16[8,128,128]{2,1,0:T(8,128)(2,1)S(1)} %fusion.46), channel_id=1, source_target_pairs={{0,128},{128,0},{4,132},{132,4},{8,136},{136,8},{12,140},{140,12},... | collective-permute-start | bytes 786440 | tf_op jit(solution)/shard_map/ppermute | solution.py:18
  133.3 11.5 %collective-permute-done.5 = bf16[8,128,128]{2,1,0:T(8,128)(2,1)S(1)} collective-permute-done((bf16[8,128,128]{2,1,0:T(8,128)(2,1)S(1)}, bf16[8,128,128]{2,1,0:T(8,128)(2,1)S(1)}, u32[]{:S(2)}, u32[]{:S(2)}) %collective-permute-start.5) | collective-permute-done | bytes 262176 | tf_op jit(solution)/shard_map/ppermute | solution.py:18
  144.9 6.4 %collective-permute-start.6 = (bf16[8,128,128]{2,1,0:T(8,128)(2,1)S(1)}, bf16[8,128,128]{2,1,0:T(8,128)(2,1)S(1)}, u32[]{:S(2)}, u32[]{:S(2)}) collective-permute-start(bf16[8,128,128]{2,1,0:T(8,128)(2,1)S(1)} %fusion.29), channel_id=1, source_target_pairs={{0,256},{256,0},{4,260},{260,4},{8,264},{264,8},{12,268},{268,12},... | collective-permute-start | bytes 786440 | tf_op jit(solution)/shard_map/ppermute | solution.py:18
  151.5 33.5 %collective-permute-done.9 = bf16[8,5,128,128]{2,3,1,0:T(8,128)(2,1)S(1)} collective-permute-done((bf16[8,5,128,128]{2,3,1,0:T(8,128)(2,1)S(1)}, bf16[8,5,128,128]{2,3,1,0:T(8,128)(2,1)S(1)}, u32[]{:S(2)}, u32[]{:S(2)}) %collective-permute-start.9) | collective-permute-done | bytes 1310752 | tf_op jit(solution)/shard_map/ppermute | solution.py:18
  186.9 6.5 %collective-permute-start.10 = (bf16[8,4,128,128]{2,3,1,0:T(8,128)(2,1)S(1)}, bf16[8,4,128,128]{2,3,1,0:T(8,128)(2,1)S(1)}, u32[]{:S(2)}, u32[]{:S(2)}) collective-permute-start(bf16[8,4,128,128]{2,3,1,0:T(8,128)(2,1)S(1)} %get-tuple-element.19), channel_id=1, source_target_pairs={{0,32},{32,0},{4,36},{36,4},{8,40},{40,8},{12,44},{44,12},{16,48},... | collective-permute-start | bytes 3145736 | tf_op jit(solution)/shard_map/ppermute | solution.py:18
  196.4 42.6 %collective-permute-done.10 = bf16[8,4,128,128]{2,3,1,0:T(8,128)(2,1)S(1)} collective-permute-done((bf16[8,4,128,128]{2,3,1,0:T(8,128)(2,1)S(1)}, bf16[8,4,128,128]{2,3,1,0:T(8,128)(2,1)S(1)}, u32[]{:S(2)}, u32[]{:S(2)}) %collective-permute-start.10) | collective-permute-done | bytes 1048608 | tf_op jit(solution)/shard_map/ppermute | solution.py:18
  239.2 1.8 fusion.107
  241.3 3.1 collective-permute-start.11
  245.9 14.7 %collective-permute-done.11 = bf16[8,3,128,128]{2,3,1,0:T(8,128)(2,1)} collective-permute-done((bf16[8,3,128,128]{2,3,1,0:T(8,128)(2,1)}, bf16[8,3,128,128]{2,3,1,0:T(8,128)(2,1)}, u32[]{:S(2)}, u32[]{:S(2)}) %collective-permute-start.11) | collective-permute-done | bytes 786464 | tf_op jit(solution)/shard_map/ppermute | solution.py:18
  264.4 4.2 %collective-permute-start.12 = (bf16[8,2,128,128]{2,3,1,0:T(8,128)(2,1)}, bf16[8,2,128,128]{2,3,1,0:T(8,128)(2,1)}, u32[]{:S(2)}, u32[]{:S(2)}) collective-permute-start(bf16[8,2,128,128]{2,3,1,0:T(8,128)(2,1)} %get-tuple-element.15), channel_id=1, source_target_pairs={{0,128},{128,0},{4,132},{132,4},{8,136},{136,8},{12,140},{140,12},... | collective-permute-start | bytes 1572872 | tf_op jit(solution)/shard_map/ppermute | solution.py:18
  270.0 2.3 fusion.73
  272.3 19.2 %collective-permute-done.12 = bf16[8,2,128,128]{2,3,1,0:T(8,128)(2,1)} collective-permute-done((bf16[8,2,128,128]{2,3,1,0:T(8,128)(2,1)}, bf16[8,2,128,128]{2,3,1,0:T(8,128)(2,1)}, u32[]{:S(2)}, u32[]{:S(2)}) %collective-permute-start.12) | collective-permute-done | bytes 524320 | tf_op jit(solution)/shard_map/ppermute | solution.py:18
  294.4 6.8 %collective-permute-start.13 = (bf16[8,1,128,128]{2,3,1,0:T(8,128)(2,1)}, bf16[8,1,128,128]{2,3,1,0:T(8,128)(2,1)}, u32[]{:S(2)}, u32[]{:S(2)}) collective-permute-start(bf16[8,1,128,128]{2,3,1,0:T(8,128)(2,1)} %fusion.30), channel_id=1, source_target_pairs={{0,256},{256,0},{4,260},{260,4},{8,264},{264,8},{12,268},{268,12},... | collective-permute-start | bytes 786440 | tf_op jit(solution)/shard_map/ppermute | solution.py:18
  310.1 2.1 fusion.34
  (141 shorter events, 36.9 us)
Async XLA Ops:
  7.2 38.4 %copy-start = (bf16[128,1024]{1,0:T(8,128)(2,1)S(1)}, bf16[128,1024]{1,0:T(8,128)(2,1)}, u32[]{:S(2)}) copy-start(bf16[128,1024]{1,0:T(8,128)(2,1)} %param.9) | copy-start | bytes 786436
  7.2 16.7 %copy-start.34 = (bf16[128,1024]{1,0:T(8,128)(2,1)S(1)}, bf16[128,1024]{1,0:T(8,128)(2,1)}, u32[]{:S(2)}) copy-start(bf16[128,1024]{1,0:T(8,128)(2,1)} %param.13) | copy-start | bytes 786436
  7.2 16.8 %copy-start.35 = (bf16[128,1024]{1,0:T(8,128)(2,1)S(1)}, bf16[128,1024]{1,0:T(8,128)(2,1)}, u32[]{:S(2)}) copy-start(bf16[128,1024]{1,0:T(8,128)(2,1)} %param.7) | copy-start | bytes 786436
  9.1 10.4 %all-to-all-start = ((bf16[512,4,64]{0,2,1:T(8,128)(2,1)}), bf16[512,4,64]{0,2,1:T(8,128)(2,1)S(1)}, u32[]{:S(2)}, u32[]{:S(2)}) async-start(bf16[512,4,64]{0,2,1:T(8,128)(2,1)} %bitcast.3), calls=%async_computation | async-start | bytes 524288 | tf_op jit(solution)/shard_map/all_to_all | solution.py:30
  20.3 10.4 %all-to-all-start.1 = ((bf16[4,128,512]{1,2,0:T(8,128)(2,1)}), bf16[4,128,512]{1,2,0:T(8,128)(2,1)S(1)}, u32[]{:S(2)}, u32[]{:S(2)}) async-start(bf16[4,128,512]{1,2,0:T(8,128)(2,1)} %stack.39), calls=%async_computation.1 | async-start | bytes 1048576 | tf_op jit(solution)/shard_map/all_to_all | solution.py:32
  23.8 283.0 %reduce-scatter.2.cloned.1.call-start = ((), (), s32[]{:S(2)}) async-start(), calls=%async_computation.3 | async-start | bytes 1310720 | tf_op jit(solution)/shard_map/reduce_scatter | solution.py:145
  24.1 38.9 %copy-start.12 = (bf16[16,8,8,128]{3,2,1,0:T(8,128)(2,1)}, bf16[16,8,8,128]{3,2,1,0:T(8,128)(2,1)S(1)}, u32[]{:S(2)}) copy-start(bf16[16,8,8,128]{3,2,1,0:T(8,128)(2,1)S(1)} %copy.102) | copy-start | bytes 786436
  24.4 11.3 %copy-start.28 = (bf16[4,8,8,512]{3,2,0,1:T(8,128)(2,1)}, bf16[4,8,8,512]{3,2,0,1:T(8,128)(2,1)S(1)}, u32[]{:S(2)}) copy-start(bf16[4,8,8,512]{3,2,0,1:T(8,128)(2,1)S(1)} %copy.101) | copy-start | bytes 786436
  32.4 12.8 %copy-start.19 = (bf16[128,1024]{1,0:T(8,128)(2,1)S(1)}, bf16[128,1024]{1,0:T(8,128)(2,1)}, u32[]{:S(2)}) copy-start(bf16[128,1024]{1,0:T(8,128)(2,1)} %param.8) | copy-start | bytes 786436
  35.7 16.3 %collective-permute-start.7 = (bf16[8,7,128,128]{2,3,1,0:T(8,128)(2,1)}, bf16[8,7,128,128]{2,3,1,0:T(8,128)(2,1)}, u32[]{:S(2)}, u32[]{:S(2)}) collective-permute-start(bf16[8,7,128,128]{2,3,1,0:T(8,128)(2,1)} %get-tuple-element.35), channel_id=1, source_target_pairs={{0,4},{4,0},{8,12},{12,8},{16,20},{20,16},{24,28},{28,24},{32,36},... | collective-permute-start | bytes 5505032 | tf_op jit(solution)/shard_map/ppermute | solution.py:18
  46.3 3.4 %collective-permute-start = (bf16[8,128,128]{2,1,0:T(8,128)(2,1)S(1)}, bf16[8,128,128]{2,1,0:T(8,128)(2,1)S(1)}, u32[]{:S(2)}, u32[]{:S(2)}) collective-permute-start(bf16[8,128,128]{2,1,0:T(8,128)(2,1)S(1)} %get-tuple-element.29), channel_id=1, source_target_pairs={{0,4},{4,0},{8,12},{12,8},{16,20},{20,16},{24,28},{28,24},{32,36},... | collective-permute-start | bytes 786440 | tf_op jit(solution)/shard_map/ppermute | solution.py:18
  49.8 10.8 %collective-permute-start.1 = (bf16[8,128,128]{2,1,0:T(8,128)(2,1)S(1)}, bf16[8,128,128]{2,1,0:T(8,128)(2,1)S(1)}, u32[]{:S(2)}, u32[]{:S(2)}) collective-permute-start(bf16[8,128,128]{2,1,0:T(8,128)(2,1)S(1)} %fusion.44), channel_id=1, source_target_pairs={{0,8},{8,0},{4,12},{12,4},{16,24},{24,16},{20,28},{28,20},{32,40},... | collective-permute-start | bytes 786440 | tf_op jit(solution)/shard_map/ppermute | solution.py:18
  57.2 58.2 %collective-permute-start.8 = (bf16[8,6,128,128]{2,3,1,0:T(8,128)(2,1)}, bf16[8,6,128,128]{2,3,1,0:T(8,128)(2,1)}, u32[]{:S(2)}, u32[]{:S(2)}) collective-permute-start(bf16[8,6,128,128]{2,3,1,0:T(8,128)(2,1)} %get-tuple-element.23), channel_id=1, source_target_pairs={{0,8},{8,0},{4,12},{12,4},{16,24},{24,16},{20,28},{28,20},{32,40},... | collective-permute-start | bytes 4718600 | tf_op jit(solution)/shard_map/ppermute | solution.py:18
  60.7 39.0 %collective-permute-start.2 = (bf16[8,128,128]{2,1,0:T(8,128)(2,1)S(1)}, bf16[8,128,128]{2,1,0:T(8,128)(2,1)S(1)}, u32[]{:S(2)}, u32[]{:S(2)}) collective-permute-start(bf16[8,128,128]{2,1,0:T(8,128)(2,1)S(1)} %fusion.105), channel_id=1, source_target_pairs={{0,16},{16,0},{4,20},{20,4},{8,24},{24,8},{12,28},{28,12},{32,48},... | collective-permute-start | bytes 786440 | tf_op jit(solution)/shard_map/ppermute | solution.py:18
  63.3 49.2 %copy-start.21 = (bf16[128,8,128]{0,2,1:T(8,128)(2,1)}, bf16[128,8,128]{0,2,1:T(8,128)(2,1)S(1)}, u32[]{:S(2)}) copy-start(bf16[128,8,128]{0,2,1:T(8,128)(2,1)S(1)} %copy.52) | copy-start | bytes 786436
  63.6 131.2 %copy-start.30 = (bf16[8,128,128]{2,1,0:T(8,128)(2,1)}, bf16[8,128,128]{2,1,0:T(8,128)(2,1)S(1)}, u32[]{:S(2)}) copy-start(bf16[8,128,128]{2,1,0:T(8,128)(2,1)S(1)} %fusion.11) | copy-start | bytes 786436
  99.7 12.7 %copy-start.23 = (bf16[8,128,128]{2,1,0:T(8,128)(2,1)}, bf16[8,128,128]{2,1,0:T(8,128)(2,1)S(1)}, u32[]{:S(2)}) copy-start(bf16[8,128,128]{2,1,0:T(8,128)(2,1)S(1)} %collective-permute-done.2) | copy-start | bytes 786436
  99.9 12.4 %collective-permute-start.3 = (bf16[8,128,128]{2,1,0:T(8,128)(2,1)S(1)}, bf16[8,128,128]{2,1,0:T(8,128)(2,1)S(1)}, u32[]{:S(2)}, u32[]{:S(2)}) collective-permute-start(bf16[8,128,128]{2,1,0:T(8,128)(2,1)S(1)} %fusion.45), channel_id=1, source_target_pairs={{0,32},{32,0},{4,36},{36,4},{8,40},{40,8},{12,44},{44,12},{16,48},... | collective-permute-start | bytes 786440 | tf_op jit(solution)/shard_map/ppermute | solution.py:18
  112.4 16.4 %collective-permute-start.4 = (bf16[8,128,128]{2,1,0:T(8,128)(2,1)S(1)}, bf16[8,128,128]{2,1,0:T(8,128)(2,1)S(1)}, u32[]{:S(2)}, u32[]{:S(2)}) collective-permute-start(bf16[8,128,128]{2,1,0:T(8,128)(2,1)S(1)} %get-tuple-element.25), channel_id=1, source_target_pairs={{0,64},{64,0},{4,68},{68,4},{8,72},{72,8},{12,76},{76,12},{16,80},... | collective-permute-start | bytes 786440 | tf_op jit(solution)/shard_map/ppermute | solution.py:18
  117.2 11.5 %copy-start.24 = (bf16[8,128,128]{2,1,0:T(8,128)(2,1)S(1)}, bf16[8,128,128]{2,1,0:T(8,128)(2,1)}, u32[]{:S(2)}) copy-start(bf16[8,128,128]{2,1,0:T(8,128)(2,1)} %copy-done.23) | copy-start | bytes 786436
  117.7 67.3 %collective-permute-start.9 = (bf16[8,5,128,128]{2,3,1,0:T(8,128)(2,1)S(1)}, bf16[8,5,128,128]{2,3,1,0:T(8,128)(2,1)S(1)}, u32[]{:S(2)}, u32[]{:S(2)}) collective-permute-start(bf16[8,5,128,128]{2,3,1,0:T(8,128)(2,1)S(1)} %get-tuple-element.21), channel_id=1, source_target_pairs={{0,16},{16,0},{4,20},{20,4},{8,24},{24,8},{12,28},{28,12},{32,48},... | collective-permute-start | bytes 3932168 | tf_op jit(solution)/shard_map/ppermute | solution.py:18
  128.9 16.0 %collective-permute-start.5 = (bf16[8,128,128]{2,1,0:T(8,128)(2,1)S(1)}, bf16[8,128,128]{2,1,0:T(8,128)(2,1)S(1)}, u32[]{:S(2)}, u32[]{:S(2)}) collective-permute-start(bf16[8,128,128]{2,1,0:T(8,128)(2,1)S(1)} %fusion.46), channel_id=1, source_target_pairs={{0,128},{128,0},{4,132},{132,4},{8,136},{136,8},{12,140},{140,12},... | collective-permute-start | bytes 786440 | tf_op jit(solution)/shard_map/ppermute | solution.py:18
  144.9 48.4 %collective-permute-start.6 = (bf16[8,128,128]{2,1,0:T(8,128)(2,1)S(1)}, bf16[8,128,128]{2,1,0:T(8,128)(2,1)S(1)}, u32[]{:S(2)}, u32[]{:S(2)}) collective-permute-start(bf16[8,128,128]{2,1,0:T(8,128)(2,1)S(1)} %fusion.29), channel_id=1, source_target_pairs={{0,256},{256,0},{4,260},{260,4},{8,264},{264,8},{12,268},{268,12},... | collective-permute-start | bytes 786440 | tf_op jit(solution)/shard_map/ppermute | solution.py:18
  186.9 52.1 %collective-permute-start.10 = (bf16[8,4,128,128]{2,3,1,0:T(8,128)(2,1)S(1)}, bf16[8,4,128,128]{2,3,1,0:T(8,128)(2,1)S(1)}, u32[]{:S(2)}, u32[]{:S(2)}) collective-permute-start(bf16[8,4,128,128]{2,3,1,0:T(8,128)(2,1)S(1)} %get-tuple-element.19), channel_id=1, source_target_pairs={{0,32},{32,0},{4,36},{36,4},{8,40},{40,8},{12,44},{44,12},{16,48},... | collective-permute-start | bytes 3145736 | tf_op jit(solution)/shard_map/ppermute | solution.py:18
  241.3 19.3 %collective-permute-start.11 = (bf16[8,3,128,128]{2,3,1,0:T(8,128)(2,1)}, bf16[8,3,128,128]{2,3,1,0:T(8,128)(2,1)}, u32[]{:S(2)}, u32[]{:S(2)}) collective-permute-start(bf16[8,3,128,128]{2,3,1,0:T(8,128)(2,1)} %get-tuple-element.17), channel_id=1, source_target_pairs={{0,64},{64,0},{4,68},{68,4},{8,72},{72,8},{12,76},{76,12},{16,80},... | collective-permute-start | bytes 2359304 | tf_op jit(solution)/shard_map/ppermute | solution.py:18
  245.9 17.1 %copy-start.10 = (f32[8,3,128,128]{2,3,1,0:T(8,128)S(1)}, f32[8,3,128,128]{2,3,1,0:T(8,128)}, u32[]{:S(2)}) copy-start(f32[8,3,128,128]{2,3,1,0:T(8,128)} %get-tuple-element.18) | copy-start | bytes 4718596
  264.4 27.1 %collective-permute-start.12 = (bf16[8,2,128,128]{2,3,1,0:T(8,128)(2,1)}, bf16[8,2,128,128]{2,3,1,0:T(8,128)(2,1)}, u32[]{:S(2)}, u32[]{:S(2)}) collective-permute-start(bf16[8,2,128,128]{2,3,1,0:T(8,128)(2,1)} %get-tuple-element.15), channel_id=1, source_target_pairs={{0,128},{128,0},{4,132},{132,4},{8,136},{136,8},{12,140},{140,12},... | collective-permute-start | bytes 1572872 | tf_op jit(solution)/shard_map/ppermute | solution.py:18
  268.6 25.0 %copy-start.16 = (f32[8,2,128,128]{2,3,1,0:T(8,128)S(1)}, f32[8,2,128,128]{2,3,1,0:T(8,128)}, u32[]{:S(2)}) copy-start(f32[8,2,128,128]{2,3,1,0:T(8,128)} %get-tuple-element.16) | copy-start | bytes 3145732
  270.0 32.0 %copy-start.32 = (bf16[8,128,128]{2,1,0:T(8,128)(2,1)}, bf16[8,128,128]{2,1,0:T(8,128)(2,1)S(1)}, u32[]{:S(2)}) copy-start(bf16[8,128,128]{2,1,0:T(8,128)(2,1)S(1)} %fusion.12) | copy-start | bytes 786436
  270.0 31.3 %copy-start.15 = (bf16[8,7,128,128]{3,2,0,1:T(8,128)(2,1)S(1)}, bf16[8,7,128,128]{3,2,0,1:T(8,128)(2,1)}, u32[]{:S(2)}) copy-start(bf16[8,7,128,128]{3,2,0,1:T(8,128)(2,1)} %copy-done.14) | copy-start | bytes 5505028
  270.0 31.3 %copy-start.27 = (bf16[128,1024]{0,1:T(8,128)(2,1)S(1)}, bf16[128,1024]{0,1:T(8,128)(2,1)}, u32[]{:S(2)}) copy-start(bf16[128,1024]{0,1:T(8,128)(2,1)} %copy-done.25) | copy-start | bytes 786436
  294.4 15.7 %collective-permute-start.13 = (bf16[8,1,128,128]{2,3,1,0:T(8,128)(2,1)}, bf16[8,1,128,128]{2,3,1,0:T(8,128)(2,1)}, u32[]{:S(2)}, u32[]{:S(2)}) collective-permute-start(bf16[8,1,128,128]{2,3,1,0:T(8,128)(2,1)} %fusion.30), channel_id=1, source_target_pairs={{0,256},{256,0},{4,260},{260,4},{8,264},{264,8},{12,268},{268,12},... | collective-permute-start | bytes 786440 | tf_op jit(solution)/shard_map/ppermute | solution.py:18
  (22 other events, 76.5 us)
Sparse Core Ops, SparseCore 0:
  246.0 26.0 reduce-scatter.1
